TPU v7x, 32 devices: a whole 2x2x4 slice. The times are simulated.
32 devices in a mesh: dp: 8 (over z, x), ctx: 2 (over y), tp: 2 (over core).
Axes of the slice: x: 2, y: 2, z: 4, core: 2. Of those that a mesh axis runs over, the one named last changes fastest.
Arguments:
- inputs: bfloat16 [4096, 768], P(('dp', 'ctx')), may hold values from -6 to 6
- qkv_weight: bfloat16 [3, 768, 768], P(None, 'dp', 'tp'), may hold values from -0.21875 to 0.21875
- out_weight: bfloat16 [768, 768], P('tp', 'dp'), may hold values from -2.5 to 2.5
- up_weight: bfloat16 [768, 3072], P('dp', 'tp'), may hold values from -0.21875 to 0.21875
- down_weight: bfloat16 [3072, 768], P('tp', 'dp'), may hold values from -0.109375 to 0.109375
- norm_gains: bfloat16 [2, 768], P(None, 'dp'), may hold values from 0.099609375 to 1.8984375
- norm_biases: bfloat16 [2, 768], P(None, 'dp'), may hold values from -3 to 3
- lengths: int32 [8, 1], P('dp'), may hold values from 4 to 8, as said below
- random_blocks: int32 [64, 12, 3], P(('dp', 'ctx'), 'tp'), may hold values from 0 to 4095
- out_grad: bfloat16 [4096, 768], P(('dp', 'ctx')), may hold values from -6 to 6
Outputs:
- output: bfloat16 [4096, 768], P(('dp', 'ctx'))
- input_grad: bfloat16 [4096, 768], P(('dp', 'ctx'))
- qkv_grad: float32 [3, 768, 768], P(None, 'dp', 'tp')
- proj_grad: float32 [768, 768], P('tp', 'dp')
- up_grad: float32 [768, 3072], P('dp', 'tp')
- down_grad: float32 [3072, 768], P('tp', 'dp')
- gains_grad: float32 [2, 768], P(None, 'dp')
- biases_grad: float32 [2, 768], P(None, 'dp')
Inputs may be any that keep to these rules, and one draw needn't show every extreme that they name: Each of a group's 1 sequence has 4 blocks or more, a group's lengths sum to 8, and the first group's first sequence has the most, 8 blocks.
All inputs are finite; a program needn't handle non-finite values.
Results may differ from a plain program's by a relative error of at most 0.02.
Values may be sent and summed in bfloat16 or wider, within the bound.
No kernel may reach another device: no remote copies, remote signals or barrier semaphores. Data moves between devices by JAX's collectives and lax.ppermute only.
A program may use at most 128 MiB of HBM per device.

v0:
```python
import math
import jax
import jax.numpy as jnp
from jax import lax
from jax.sharding import PartitionSpec as P

HD = 64
BLOCK = 64
eps = 1e-06


def layer_norm(values, gain, shift):
    row_mean = jnp.mean(values, axis=-1, keepdims=True)
    centred = values - row_mean
    spread = jnp.mean(centred * centred, axis=-1, keepdims=True)
    return centred * lax.rsqrt(spread + eps) * gain + shift


def gelu_tanh(values):
    return jax.nn.gelu(values, approximate=True)


def contract(form, left, right):
    return jnp.einsum(form, left, right, preferred_element_type=jnp.float32)


def block_table(blocks, lengths_row, offsets):
    seq_ends = jnp.cumsum(lengths_row)
    starts = seq_ends - lengths_row
    inside = ((blocks[:, None] >= starts[None, :]) & (blocks[:, None] < seq_ends[None, :])).astype(
        jnp.int32
    )
    seq_first = jnp.sum(inside * starts[None, :], axis=1)
    seq_count = jnp.sum(inside * lengths_row[None, :], axis=1)
    position = blocks - seq_first
    has_before = position > 0
    has_behind = position < seq_count - 1
    before = jnp.where(has_before, blocks - 1, blocks)
    behind = jnp.where(has_behind, blocks + 1, blocks)
    fixed_ids = jnp.stack([before, blocks, behind, seq_first, seq_first + 1], axis=-1)
    random_ids = seq_first[:, None, None] + offsets % seq_count[:, None, None]
    head_count = offsets.shape[1]
    key_table = jnp.concatenate(
        [jnp.broadcast_to(fixed_ids[:, None, :], (blocks.shape[0], head_count, 5)), random_ids],
        axis=-1,
    )
    always = jnp.ones_like(has_before)
    usable = jnp.stack(
        [has_before, always, has_behind, always, always] + [always] * offsets.shape[2], axis=-1
    )
    return (key_table, usable)


def scores_of(query, key_sel, usable, scale):
    raw = contract("bqhd,bhkcd->bhqkc", query, key_sel)
    return jnp.where(usable[:, None, None, :, None], raw * scale, -1e30)


def per_device(
    inputs,
    qkv_weight,
    out_weight,
    up_weight,
    down_weight,
    norm_gains,
    norm_biases,
    lengths,
    random_blocks,
    out_grad,
):
    w_qkv, w_out, w_up, w_down, gains_low, biases_low = (
        lax.all_gather(qkv_weight, "dp", axis=1, tiled=True),
        lax.all_gather(out_weight, "dp", axis=1, tiled=True),
        lax.all_gather(up_weight, "dp", axis=0, tiled=True),
        lax.all_gather(down_weight, "dp", axis=1, tiled=True),
        lax.all_gather(norm_gains, "dp", axis=1, tiled=True),
        lax.all_gather(norm_biases, "dp", axis=1, tiled=True),
    )
    gains = gains_low.astype(jnp.float32)
    biases = biases_low.astype(jnp.float32)
    rows = inputs.shape[0]
    own_blocks = rows // BLOCK
    local_width = w_qkv.shape[2]
    local_heads = local_width // HD
    scale = 1.0 / math.sqrt(HD)
    x_float = inputs.astype(jnp.float32)
    projected = contract("td,kde->kte", inputs, w_qkv)
    q_low = projected[0].astype(jnp.bfloat16)
    k_low = projected[1].astype(jnp.bfloat16)
    v_low = projected[2].astype(jnp.bfloat16)
    key_all, value_all = (
        lax.all_gather(k_low, "ctx", axis=0, tiled=True),
        lax.all_gather(v_low, "ctx", axis=0, tiled=True),
    )
    group_blocks = key_all.shape[0] // BLOCK
    first_block = lax.axis_index("ctx") * own_blocks
    blocks = first_block + jnp.arange(own_blocks, dtype=jnp.int32)
    key_table, usable = block_table(blocks, lengths[0], random_blocks)
    head_pick = jnp.arange(local_heads, dtype=jnp.int32)[None, :, None]
    key_blocks = key_all.reshape(group_blocks, BLOCK, local_heads, HD)
    value_blocks = value_all.reshape(group_blocks, BLOCK, local_heads, HD)
    key_sel = key_blocks[key_table, :, head_pick, :]
    value_sel = value_blocks[key_table, :, head_pick, :]
    query = q_low.reshape(own_blocks, BLOCK, local_heads, HD)
    scores = scores_of(query, key_sel, usable, scale)
    top = jnp.max(scores, axis=(3, 4), keepdims=True)
    log_total = top + jnp.log(jnp.sum(jnp.exp(scores - top), axis=(3, 4), keepdims=True))
    probs = jnp.exp(scores - log_total)
    probs_low = probs.astype(jnp.bfloat16)
    attended = (
        contract("bhqkc,bhkcd->bqhd", probs_low, value_sel)
        .reshape(rows, local_width)
        .astype(jnp.bfloat16)
    )
    attn_sum = lax.psum(
        jnp.dot(attended, w_out, preferred_element_type=jnp.float32).astype(jnp.bfloat16), "tp"
    ).astype(jnp.float32)
    first_sum = x_float + attn_sum
    normed, norm_pull = jax.vjp(layer_norm, first_sum, gains[0], biases[0])
    normed_low = normed.astype(jnp.bfloat16)
    hidden = jnp.dot(normed_low, w_up, preferred_element_type=jnp.float32)
    activated, gelu_pull = jax.vjp(gelu_tanh, hidden)
    act_low = activated.astype(jnp.bfloat16)
    mlp_sum = lax.psum(
        jnp.dot(act_low, w_down, preferred_element_type=jnp.float32).astype(jnp.bfloat16), "tp"
    ).astype(jnp.float32)
    second_sum = normed + mlp_sum
    result, final_pull = jax.vjp(layer_norm, second_sum, gains[1], biases[1])
    d_second, d_gain_two, d_bias_two = final_pull(out_grad.astype(jnp.float32))
    d_mlp = d_second.astype(jnp.bfloat16)
    grad_down = contract("tf,td->fd", act_low, d_mlp)
    d_act = contract("td,fd->tf", d_mlp, w_down)
    d_hidden = gelu_pull(d_act)[0].astype(jnp.bfloat16)
    grad_up = contract("td,tf->df", normed_low, d_hidden)
    d_normed = d_second + lax.psum(
        contract("tf,df->td", d_hidden, w_up).astype(jnp.bfloat16), "tp"
    ).astype(jnp.float32)
    d_first, d_gain_one, d_bias_one = norm_pull(d_normed)
    d_attn = d_first.astype(jnp.bfloat16)
    grad_proj = contract("te,td->ed", attended, d_attn)
    d_attended = (
        contract("td,ed->te", d_attn, w_out)
        .astype(jnp.bfloat16)
        .reshape(own_blocks, BLOCK, local_heads, HD)
    )
    scores = scores_of(query, key_sel, usable, scale)
    probs = jnp.exp(scores - log_total)
    probs_low = probs.astype(jnp.bfloat16)
    d_probs = contract("bqhd,bhkcd->bhqkc", d_attended, value_sel)
    d_scores = probs * (d_probs - jnp.sum(probs * d_probs, axis=(3, 4), keepdims=True))
    d_raw = (d_scores * scale).astype(jnp.bfloat16)
    d_query = (
        contract("bhqkc,bhkcd->bqhd", d_raw, key_sel)
        .reshape(rows, local_width)
        .astype(jnp.bfloat16)
    )
    d_key_sel = contract("bhqkc,bqhd->bhkcd", d_raw, query)
    d_value_sel = contract("bhqkc,bqhd->bhkcd", probs_low, d_attended)
    empty = jnp.zeros((group_blocks, BLOCK, local_heads, HD), jnp.float32)
    d_key_all = (
        empty.at[key_table, :, head_pick, :]
        .add(d_key_sel)
        .reshape(group_blocks * BLOCK, local_width)
    )
    d_value_all = (
        empty.at[key_table, :, head_pick, :]
        .add(d_value_sel)
        .reshape(group_blocks * BLOCK, local_width)
    )
    d_key, d_value = (
        lax.psum_scatter(
            d_key_all.astype(jnp.bfloat16), "ctx", scatter_dimension=0, tiled=True
        ).astype(jnp.float32),
        lax.psum_scatter(
            d_value_all.astype(jnp.bfloat16), "ctx", scatter_dimension=0, tiled=True
        ).astype(jnp.float32),
    )
    d_projected = jnp.stack([d_query, d_key.astype(jnp.bfloat16), d_value.astype(jnp.bfloat16)])
    grad_qkv = contract("td,kte->kde", inputs, d_projected)
    d_inputs = d_first + lax.psum(
        contract("kte,kde->td", d_projected, w_qkv).astype(jnp.bfloat16), "tp"
    ).astype(jnp.float32)
    grad_gains = jnp.stack([d_gain_one, d_gain_two])
    grad_biases = jnp.stack([d_bias_one, d_bias_two])
    shared = (
        lax.psum_scatter(
            grad_qkv.astype(jnp.bfloat16), "dp", scatter_dimension=1, tiled=True
        ).astype(jnp.float32),
        lax.psum_scatter(
            grad_proj.astype(jnp.bfloat16), "dp", scatter_dimension=1, tiled=True
        ).astype(jnp.float32),
        lax.psum_scatter(
            grad_up.astype(jnp.bfloat16), "dp", scatter_dimension=0, tiled=True
        ).astype(jnp.float32),
        lax.psum_scatter(
            grad_down.astype(jnp.bfloat16), "dp", scatter_dimension=1, tiled=True
        ).astype(jnp.float32),
        lax.psum_scatter(
            grad_gains.astype(jnp.bfloat16), "dp", scatter_dimension=1, tiled=True
        ).astype(jnp.float32),
        lax.psum_scatter(
            grad_biases.astype(jnp.bfloat16), "dp", scatter_dimension=1, tiled=True
        ).astype(jnp.float32),
    )
    totals = (
        lax.psum(shared[0].astype(jnp.bfloat16), "ctx").astype(jnp.float32),
        lax.psum(shared[1].astype(jnp.bfloat16), "ctx").astype(jnp.float32),
        lax.psum(shared[2].astype(jnp.bfloat16), "ctx").astype(jnp.float32),
        lax.psum(shared[3].astype(jnp.bfloat16), "ctx").astype(jnp.float32),
        lax.psum(shared[4].astype(jnp.bfloat16), "ctx").astype(jnp.float32),
        lax.psum(shared[5].astype(jnp.bfloat16), "ctx").astype(jnp.float32),
    )
    return (
        result.astype(jnp.bfloat16),
        d_inputs.astype(jnp.bfloat16),
        totals[0],
        totals[1],
        totals[2],
        totals[3],
        totals[4],
        totals[5],
    )


def solution(mesh):
    return jax.shard_map(
        per_device,
        mesh=mesh,
        in_specs=(
            P(("dp", "ctx"), None),
            P(None, "dp", "tp"),
            P("tp", "dp"),
            P("dp", "tp"),
            P("tp", "dp"),
            P(None, "dp"),
            P(None, "dp"),
            P("dp", None),
            P(("dp", "ctx"), "tp", None),
            P(("dp", "ctx"), None),
        ),
        out_specs=(
            P(("dp", "ctx"), None),
            P(("dp", "ctx"), None),
            P(None, "dp", "tp"),
            P("tp", "dp"),
            P("dp", "tp"),
            P("tp", "dp"),
            P(None, "dp"),
            P(None, "dp"),
        ),
        check_vma=False,
    )
```

profile of v0, /device:TPU:0, one launch (start us, length us, event | category | flops | bytes accessed | tf_op | source)
XLA Modules:
  0.0 850.2 jit_solution(17683783043665351817)
XLA Ops:
  10.7 36.1 %all_gather.27 = bf16[384,768]{0,1:T(8,128)(2,1)} all-gather(bf16[384,96]{0,1:T(8,128)(2,1)} %param.12), channel_id=1, replica_groups=mesh['dp'=8,'ctx'=2,'tp'=2] {'dp'}, dimensions={1}, use_global_device_ids=true | all-gather | bytes 663552 | tf_op jit(solution)/shard_map/all_gather | solution.py:73
  46.8 13.7 %all-gather.8.cloned.1.call-done = bf16[3,768,384]{2,1,0:T(8,128)(2,1)} async-done(((bf16[3,96,384]{2,1,0:T(8,128)(2,1)}), bf16[3,768,384]{2,1,0:T(8,128)(2,1)}) %all-gather.8.cloned.1.call-update) | async-done | bytes 1769488 | tf_op jit(solution)/shard_map/all_gather | solution.py:72
  60.5 2.2 fusion.12
  63.5 6.8 all-gather.1
  72.6 3.4 gather_fusion.1
  77.7 1.6 exponential_reduce_fusion
  80.3 6.8 all-gather
  88.2 3.7 gather_fusion
  91.8 5.6 fusion.14
  100.7 19.4 %all-gather.2 = bf16[8,96,2]{1,2,0:T(2,128)(2,1)S(1)} all-gather(bf16[1,96,2]{1,2,0:T(2,128)(2,1)S(1)} %bitcast.123), channel_id=1, replica_groups=mesh['dp'=8,'ctx'=2,'tp'=2] {'dp'}, dimensions={0}, use_global_device_ids=true | all-gather | bytes 3456 | tf_op jit(solution)/shard_map/all_gather | solution.py:76
  120.2 16.2 %all-gather.3 = bf16[8,96,2]{1,2,0:T(2,128)(2,1)S(1)} all-gather(bf16[1,96,2]{1,2,0:T(2,128)(2,1)S(1)} %bitcast.124), channel_id=1, replica_groups=mesh['dp'=8,'ctx'=2,'tp'=2] {'dp'}, dimensions={0}, use_global_device_ids=true | all-gather | bytes 3456 | tf_op jit(solution)/shard_map/all_gather | solution.py:77
  138.9 34.7 %all-gather.10.cloned.1.call-done = bf16[768,1536]{1,0:T(8,128)(2,1)} async-done(((bf16[96,1536]{1,0:T(8,128)(2,1)}), bf16[768,1536]{1,0:T(8,128)(2,1)}) %all-gather.10.cloned.1.call-update) | async-done | bytes 2359312 | tf_op jit(solution)/shard_map/all_gather | solution.py:74
  173.7 2.7 fusion.46
  176.4 50.2 %all-gather.12.cloned.1.call-done = bf16[1536,768]{0,1:T(8,128)(2,1)} async-done(((bf16[1536,96]{0,1:T(8,128)(2,1)}), bf16[1536,768]{0,1:T(8,128)(2,1)}) %all-gather.12.cloned.1.call-update) | async-done | bytes 2359312 | tf_op jit(solution)/shard_map/all_gather | solution.py:75
  226.6 3.5 convolution_convert_fusion.5
  230.2 17.1 %all-reduce.10.cloned.1.call-done = bf16[256,768]{1,0:T(8,128)(2,1)} async-done(((bf16[256,768]{1,0:T(8,128)(2,1)}), bf16[256,768]{1,0:T(8,128)(2,1)}) %all-reduce.10.cloned.1.call-update) | async-done | bytes 393232 | tf_op jit(solution)/shard_map/psum | solution.py:124
  253.0 1.6 convolution_convert_fusion.4
  254.9 19.5 %all-reduce.12.cloned.1.call-done = bf16[256,768]{1,0:T(8,128)(2,1)} async-done(((bf16[256,768]{1,0:T(8,128)(2,1)}), bf16[256,768]{1,0:T(8,128)(2,1)}) %all-reduce.12.cloned.1.call-update) | async-done | bytes 393232 | tf_op jit(solution)/shard_map/psum | solution.py:135
  274.4 2.1 multiply_reduce_fusion.1
  276.6 1.5 fusion.51
  280.1 5.8 multiply_reduce_fusion
  286.0 2.1 multiply_convert_fusion
  288.2 3.6 fusion.55
  292.0 21.6 %scatter_fusion = f32[8,64,6,64]{3,1,2,0:T(8,128)S(1)} fusion(f32[8,64,6,64]{3,1,2,0:T(8,128)S(1)} %broadcast_in_dim.38.clone.1, s32[192]{0:T(256)S(1)} %reshape.312, f32[192,64,64]{2,1,0:T(8,128)} %bitcast.109), kind=kCustom, calls=%fused_computation.2 | custom fusion | flops 786432 | bytes 9438720 | tf_op jit(solution)/shard_map/scatter-add | solution.py:162
  315.7 6.8 fusion.24
  322.7 21.7 %scatter_fusion.1 = f32[8,64,6,64]{3,1,2,0:T(8,128)S(1)} fusion(f32[8,64,6,64]{3,1,2,0:T(8,128)S(1)} %broadcast_in_dim.38.clone, s32[192]{0:T(256)S(1)} %reshape.312, f32[192,64,64]{2,1,0:T(8,128)} %bitcast.108), kind=kCustom, calls=%fused_computation.3 | custom fusion | flops 786432 | bytes 9438720 | tf_op jit(solution)/shard_map/scatter-add | solution.py:167
  346.1 2.5 reshape.344
  348.8 3.8 fusion.13
  354.3 8.7 %reduce-scatter.17.cloned.1.call-done = bf16[256,384]{1,0:T(8,128)(2,1)} async-done(((bf16[512,384]{1,0:T(8,128)(2,1)}), bf16[256,384]{1,0:T(8,128)(2,1)}) %reduce-scatter.17.cloned.1.call-update) | async-done | bytes 196624 | tf_op jit(solution)/shard_map/reduce_scatter | solution.py:174
  363.0 1.7 convert_bitcast_fusion
  364.7 3.4 copy.124
  368.1 3.3 copy.133
  372.9 3.8 convolution_convert_fusion
  378.0 2.4 convolution_convert_fusion.1
  382.9 3.0 fusion.9
  386.0 51.5 %reduce-scatter.25.cloned.1.call-done = bf16[96,1152]{1,0:T(8,128)(2,1)} async-done(((bf16[768,1152]{1,0:T(8,128)(2,1)}), bf16[96,1152]{1,0:T(8,128)(2,1)}) %reduce-scatter.25.cloned.1.call-update) | async-done | bytes 221200
  439.4 62.8 %reduce-scatter.19.cloned.1.call-done = bf16[384,96]{0,1:T(8,128)(2,1)} async-done(((bf16[384,768]{0,1:T(8,128)(2,1)}), bf16[384,96]{0,1:T(8,128)(2,1)}) %reduce-scatter.19.cloned.1.call-update) | async-done | bytes 73744 | tf_op jit(solution)/shard_map/reduce_scatter | solution.py:189
  502.2 72.0 %reduce-scatter.23.cloned.1.call-done = bf16[1536,96]{0,1:T(8,128)(2,1)} async-done(((bf16[1536,768]{0,1:T(8,128)(2,1)}), bf16[1536,96]{0,1:T(8,128)(2,1)}) %reduce-scatter.23.cloned.1.call-update) | async-done | bytes 294928 | tf_op jit(solution)/shard_map/reduce_scatter | solution.py:195
  574.2 71.9 %reduce-scatter.21.cloned.1.call-done = bf16[96,1536]{1,0:T(8,128)(2,1)} async-done(((bf16[768,1536]{1,0:T(8,128)(2,1)}), bf16[96,1536]{1,0:T(8,128)(2,1)}) %reduce-scatter.21.cloned.1.call-update) | async-done | bytes 294928 | tf_op jit(solution)/shard_map/reduce_scatter | solution.py:192
  646.0 64.3 %reduce-scatter.27.cloned.1.call-done = bf16[96,2]{1,0:T(8,128)(2,1)} async-done(((bf16[768,2]{1,0:T(8,128)(2,1)}), bf16[96,2]{1,0:T(8,128)(2,1)}) %reduce-scatter.27.cloned.1.call-update) | async-done | bytes 400
  711.2 62.8 %reduce-scatter.29.cloned.1.call-done = bf16[96,2]{1,0:T(8,128)(2,1)} async-done(((bf16[768,2]{1,0:T(8,128)(2,1)}), bf16[96,2]{1,0:T(8,128)(2,1)}) %reduce-scatter.29.cloned.1.call-update) | async-done | bytes 400
  774.8 4.9 all-reduce
  780.9 13.5 %all-reduce.14.cloned.1.call-done = bf16[256,768]{1,0:T(8,128)(2,1)} async-done(((bf16[256,768]{1,0:T(8,128)(2,1)}), bf16[256,768]{1,0:T(8,128)(2,1)}) %all-reduce.14.cloned.1.call-update) | async-done | bytes 393232 | tf_op jit(solution)/shard_map/psum | solution.py:180
  794.4 1.9 add_convert_fusion
  796.3 40.9 %all-reduce.16.cloned.1.call-done = (bf16[3,96,384]{1,2,0:T(8,128)(2,1)}, bf16[384,96]{0,1:T(8,128)(2,1)}, bf16[96,1536]{1,0:T(8,128)(2,1)}, bf16[1536,96]{0,1:T(8,128)(2,1)}) async-done(((bf16[3,96,384]{1,2,0:T(8,128)(2,1)}, bf16[384,96]{0,1:T(8,128)(2,1)}, bf16[96,1536]{1,0:T(8,128)(2,1)}, bf16[1536,96]{0,1:T(8,128)(2,1)}), (bf16[3,96,384]{1,2,0:T(8,128)(2,1)}, bf16[384,96]{0,1:T(8,128)(2,1)}, ...) | async-done | bytes 884752 | tf_op jit(solution)/shard_map/psum | solution.py:206
  837.2 1.9 convert_element_type.210
  839.0 1.8 convert_element_type.212
  840.8 1.9 copy.101
  (197 shorter events, 39.9 us)
Async XLA Ops:
  7.2 53.4 %all-gather.8.cloned.1.call-start = ((), (), s32[]{:S(2)}) async-start(), calls=%async_computation.8 | async-start | bytes 1990656 | tf_op jit(solution)/shard_map/all_gather | solution.py:72
  7.9 128.6 %all-reduce.8.cloned.1.call-start = ((), (), s32[]{:S(2)}) async-start(), calls=%async_computation.9 | async-start | bytes 786432 | tf_op jit(solution)/shard_map/psum | solution.py:115
  72.6 3.4 copy-start.12
  77.7 2.6 copy-start
  77.7 2.7 copy-start.20
  91.8 6.2 copy-start.11
  97.4 3.2 copy-start.32
  97.5 22.7 %copy-start.33 = (bf16[2,96]{1,0:T(2,128)(2,1)S(1)}, bf16[2,96]{1,0:T(2,128)(2,1)}, u32[]{:S(2)}) copy-start(bf16[2,96]{1,0:T(2,128)(2,1)} %param.16) | copy-start | bytes 1156
  97.5 39.0 %copy-start.4 = (bf16[256,768]{1,0:T(8,128)(2,1)S(1)}, bf16[256,768]{1,0:T(8,128)(2,1)}, u32[]{:S(2)}) copy-start(bf16[256,768]{1,0:T(8,128)(2,1)} %param.10) | copy-start | bytes 1179652
  98.1 78.3 %copy-start.16 = (bf16[256,384]{0,1:T(8,128)(2,1)}, bf16[256,384]{0,1:T(8,128)(2,1)S(1)}, u32[]{:S(2)}) copy-start(bf16[256,384]{0,1:T(8,128)(2,1)S(1)} %convert_element_type.176) | copy-start | bytes 589828
  99.3 74.4 %all-gather.10.cloned.1.call-start = ((), (), s32[]{:S(2)}) async-start(), calls=%async_computation.10 | async-start | bytes 2654208 | tf_op jit(solution)/shard_map/all_gather | solution.py:74
  100.0 126.6 %all-gather.12.cloned.1.call-start = ((), (), s32[]{:S(2)}) async-start(), calls=%async_computation.11 | async-start | bytes 2654208 | tf_op jit(solution)/shard_map/all_gather | solution.py:75
  100.6 146.7 %all-reduce.10.cloned.1.call-start = ((), (), s32[]{:S(2)}) async-start(), calls=%async_computation.12 | async-start | bytes 786432 | tf_op jit(solution)/shard_map/psum | solution.py:124
  138.9 137.6 %copy-start.23 = (f32[256]{0:T(256)}, f32[256]{0:T(256)S(1)}, u32[]{:S(2)}) copy-start(f32[256]{0:T(256)S(1)} %fusion.36) | copy-start | bytes 3076
  176.3 50.2 %copy-start.38 = (f32[256,1536]{1,0:T(8,128)}, f32[256,1536]{1,0:T(8,128)S(1)}, u32[]{:S(2)}) copy-start(f32[256,1536]{1,0:T(8,128)S(1)} %fusion.46) | copy-start | bytes 4718596
  176.4 70.9 %copy-start.5 = (bf16[256,768]{1,0:T(8,128)(2,1)S(1)}, bf16[256,768]{1,0:T(8,128)(2,1)}, u32[]{:S(2)}) copy-start(bf16[256,768]{1,0:T(8,128)(2,1)} %all-reduce.8.cloned.1.call-done) | copy-start | bytes 1179652
  230.1 18.9 %copy-start.14 = (bf16[256,768]{1,0:T(8,128)(2,1)S(1)}, bf16[256,768]{1,0:T(8,128)(2,1)}, u32[]{:S(2)}) copy-start(bf16[256,768]{1,0:T(8,128)(2,1)} %param.19) | copy-start | bytes 1179652
  230.1 44.3 %all-reduce.12.cloned.1.call-start = ((), (), s32[]{:S(2)}) async-start(), calls=%async_computation.13 | async-start | bytes 786432 | tf_op jit(solution)/shard_map/psum | solution.py:135
  248.7 2.4 copy-start.35
  248.7 2.4 copy-start.39
  251.0 25.5 %copy-start.9 = (f32[256,768]{1,0:T(8,128)}, f32[256,768]{1,0:T(8,128)S(1)}, u32[]{:S(2)}) copy-start(f32[256,768]{1,0:T(8,128)S(1)} %get-tuple-element.58) | copy-start | bytes 2359300
  251.0 25.5 %copy-start.27 = (f32[256]{0:T(256)}, f32[256]{0:T(256)S(1)}, u32[]{:S(2)}) copy-start(f32[256]{0:T(256)S(1)} %negate_multiply_fusion.1) | copy-start | bytes 3076
  251.1 1.9 copy-start.34
  253.0 23.5 %copy-start.18 = (bf16[256,1536]{1,0:T(8,128)(2,1)}, bf16[256,1536]{1,0:T(8,128)(2,1)S(1)}, u32[]{:S(2)}) copy-start(bf16[256,1536]{1,0:T(8,128)(2,1)S(1)} %fusion.8) | copy-start | bytes 2359300
  253.0 1.8 copy-start.22
  254.6 99.7 %reduce-scatter.15.cloned.1.call-start = ((), (), s32[]{:S(2)}) async-start(), calls=%async_computation.14 | async-start | bytes 589824 | tf_op jit(solution)/shard_map/reduce_scatter | solution.py:171
  278.1 1.7 copy-start.25
  279.8 6.2 slice-start
  280.1 5.9 slice-start.1
  286.0 2.2 copy-start.13
  288.2 3.6 copy-start.3
  315.7 47.3 %reduce-scatter.17.cloned.1.call-start = ((), (), s32[]{:S(2)}) async-start(), calls=%async_computation.15 | async-start | bytes 589824 | tf_op jit(solution)/shard_map/reduce_scatter | solution.py:174
  344.5 4.3 copy-start.2
  348.6 88.9 %reduce-scatter.25.cloned.1.call-start = ((), (), s32[]{:S(2)}) async-start(), calls=%async_computation.20 | async-start | bytes 1990656
  368.1 3.4 copy-start.8
  368.1 3.4 copy-start.17
  368.1 3.4 copy-start.26
  371.4 130.7 %reduce-scatter.19.cloned.1.call-start = ((), (), s32[]{:S(2)}) async-start(), calls=%async_computation.17 | async-start | bytes 663552 | tf_op jit(solution)/shard_map/reduce_scatter | solution.py:189
  372.8 201.3 %reduce-scatter.23.cloned.1.call-start = ((), (), s32[]{:S(2)}) async-start(), calls=%async_computation.19 | async-start | bytes 2654208 | tf_op jit(solution)/shard_map/reduce_scatter | solution.py:195
  376.8 3.7 copy-start.15
  376.8 269.2 %reduce-scatter.21.cloned.1.call-start = ((), (), s32[]{:S(2)}) async-start(), calls=%async_computation.18 | async-start | bytes 2654208 | tf_op jit(solution)/shard_map/reduce_scatter | solution.py:192
  380.4 2.6 copy-start.36
  380.4 2.6 copy-start.37
  380.4 330.0 %reduce-scatter.27.cloned.1.call-start = ((), (), s32[]{:S(2)}) async-start(), calls=%async_computation.21 | async-start | bytes 221184
  381.9 392.0 %reduce-scatter.29.cloned.1.call-start = ((), (), s32[]{:S(2)}) async-start(), calls=%async_computation.22 | async-start | bytes 221184
  382.9 411.5 %all-reduce.14.cloned.1.call-start = ((), (), s32[]{:S(2)}) async-start(), calls=%async_computation.16 | async-start | bytes 786432 | tf_op jit(solution)/shard_map/psum | solution.py:180
  385.9 451.2 %all-reduce.16.cloned.1.call-start = ((), (), s32[]{:S(2)}) async-start(), calls=%async_computation.23 | async-start | bytes 1916928 | tf_op jit(solution)/shard_map/psum | solution.py:206
  837.2 5.6 copy-start.21
  (10 other events, 11.9 us)
Sparse Core Ops, SparseCore 0:
  10.2 50.3 all-gather.7
  99.4 18.4 all-reduce.7
  120.4 53.2 all-gather.9
  175.9 50.6 all-gather.11
  230.2 17.0 all-reduce.9
  254.7 19.6 all-reduce.11
  315.8 14.2 reduce-scatter.14
  348.7 14.2 reduce-scatter.16
  371.6 65.8 reduce-scatter.24
  441.1 60.9 reduce-scatter.18
  506.1 68.0 reduce-scatter.22
  577.9 68.0 reduce-scatter.20
  650.2 60.1 reduce-scatter.26
  713.8 60.0 reduce-scatter.28
  776.9 17.4 all-reduce.13
  797.3 39.7 all-reduce.15
where the time goes:
time: 858 us; the launch traced here: 850 us
  waiting for transfers between devices  586 us (68%)
  blocking collectives  90.2 us (11%)
  other arithmetic  66.2 us (8%)
  matrix products  51.8 us (6%)
  local copies, waits for them, and re-layouts  39.5 us (5%)
  between operations  15.6 us (2%)
    unnamed x19, waiting for transfers between devices  181 us
    reduce_scatter x1, waiting for transfers between devices, per_device(): lax.psum_scatter(grad_down.astype(jnp.bfloat16), 'dp', scatter_dimension=...  72 us
    reduce_scatter x1, waiting for transfers between devices, per_device(): lax.psum_scatter(grad_up.astype(jnp.bfloat16), 'dp', scatter_dimension=0,...  71.9 us
    reduce_scatter x1, waiting for transfers between devices, per_device(): lax.psum_scatter(grad_proj.astype(jnp.bfloat16), 'dp', scatter_dimension=...  62.8 us
    all_gather x1, waiting for transfers between devices, per_device(): lax.all_gather(down_weight, 'dp', axis=1, tiled=True)  50.2 us
    dot_general x15, matrix products, contract(): return jnp.einsum(form, left, right, preferred_element_type=jnp.float32)  44.5 us
    psum x1, waiting for transfers between devices, per_device(): lax.psum(shared[0].astype(jnp.bfloat16), 'ctx').astype(jnp.float32)  40.9 us
    all_gather x1, blocking collectives, per_device(): lax.all_gather(out_weight, 'dp', axis=1, tiled=True)  36.1 us
  transfers between devices with their start and end apart: 16, of which 14 were waited for; matrix products, arithmetic and copies ran while one was open for 8% of the time, Pallas kernels for 0%

commit v1 on v0

--- a/solution.py
+++ b/solution.py
@@ -132,8 +132,8 @@
     d_act = contract("td,fd->tf", d_mlp, w_down)
     d_hidden = gelu_pull(d_act)[0].astype(jnp.bfloat16)
     grad_up = contract("td,tf->df", normed_low, d_hidden)
-    d_normed = d_second + lax.psum(
-        contract("tf,df->td", d_hidden, w_up).astype(jnp.bfloat16), "tp"
+    d_normed = d_second + jnp.sum(
+        lax.all_gather(contract("tf,df->td", d_hidden, w_up).astype(jnp.bfloat16), "tp"), axis=0
     ).astype(jnp.float32)
     d_first, d_gain_one, d_bias_one = norm_pull(d_normed)
     d_attn = d_first.astype(jnp.bfloat16)

time: 858 us -> 838 us (0.977)
  waiting for transfers between devices: 586 us -> 565 us
    psum x1 -> x0, waiting for transfers between devices: 19.5 us -> none  [per_device(): lax.psum(contract('tf,df->td', d_hidden, w_up).astype(jnp.bfloat16), 'tp')]
    unnamed x19 -> x18, waiting for transfers between devices: 181 us -> 180 us
  transfers between devices with their start and end apart: 16 -> 15, of which waited for: 14 -> 13; matrix products, arithmetic and copies ran while one was open for 8% -> 8% of each run, Pallas kernels for 0% -> 0%
where the time goes in v1:
time: 838 us; the launch traced here: 830 us
  waiting for transfers between devices  565 us (67%)
  blocking collectives  92.8 us (11%)
  other arithmetic  64.3 us (8%)
  matrix products  51.1 us (6%)
  local copies, waits for them, and re-layouts  40 us (5%)
  between operations  15.6 us (2%)
    unnamed x18, waiting for transfers between devices  180 us
    reduce_scatter x1, waiting for transfers between devices, per_device(): lax.psum_scatter(grad_up.astype(jnp.bfloat16), 'dp', scatter_dimension=0,...  71.5 us
    reduce_scatter x1, waiting for transfers between devices, per_device(): lax.psum_scatter(grad_down.astype(jnp.bfloat16), 'dp', scatter_dimension=...  71.4 us
    reduce_scatter x1, waiting for transfers between devices, per_device(): lax.psum_scatter(grad_proj.astype(jnp.bfloat16), 'dp', scatter_dimension=...  63.3 us
    all_gather x1, waiting for transfers between devices, per_device(): lax.all_gather(down_weight, 'dp', axis=1, tiled=True)  50.2 us
    dot_general x15, matrix products, contract(): return jnp.einsum(form, left, right, preferred_element_type=jnp.float32)  43.8 us
    psum x1, waiting for transfers between devices, per_device(): lax.psum(shared[0].astype(jnp.bfloat16), 'ctx').astype(jnp.float32)  41 us
    all_gather x1, blocking collectives, per_device(): lax.all_gather(out_weight, 'dp', axis=1, tiled=True)  36.1 us
  transfers between devices with their start and end apart: 15, of which 13 were waited for; matrix products, arithmetic and copies ran while one was open for 8% of the time, Pallas kernels for 0%

profile of v1, /device:TPU:0, one launch (start us, length us, event | category | flops | bytes accessed | tf_op | source)
XLA Modules:
  0.0 830.0 jit_solution(6687458194549011150)
XLA Ops:
  10.7 36.1 %all_gather.33 = bf16[384,768]{0,1:T(8,128)(2,1)} all-gather(bf16[384,96]{0,1:T(8,128)(2,1)} %param.12), channel_id=1, replica_groups=mesh['dp'=8,'ctx'=2,'tp'=2] {'dp'}, dimensions={1}, use_global_device_ids=true | all-gather | bytes 663552 | tf_op jit(solution)/shard_map/all_gather | solution.py:73
  46.8 13.7 %all-gather.9.cloned.1.call-done = bf16[3,768,384]{2,1,0:T(8,128)(2,1)} async-done(((bf16[3,96,384]{2,1,0:T(8,128)(2,1)}), bf16[3,768,384]{2,1,0:T(8,128)(2,1)}) %all-gather.9.cloned.1.call-update) | async-done | bytes 1769488 | tf_op jit(solution)/shard_map/all_gather | solution.py:72
  60.5 2.2 fusion.12
  63.5 6.8 all-gather.1
  70.7 1.4 copy.81
  72.6 3.4 gather_fusion.1
  77.7 1.6 exponential_reduce_fusion
  80.4 6.8 all-gather
  88.2 3.7 gather_fusion
  91.9 5.6 fusion.14
  100.7 19.4 %all-gather.3 = bf16[8,96,2]{1,2,0:T(2,128)(2,1)S(1)} all-gather(bf16[1,96,2]{1,2,0:T(2,128)(2,1)S(1)} %bitcast.125), channel_id=1, replica_groups=mesh['dp'=8,'ctx'=2,'tp'=2] {'dp'}, dimensions={0}, use_global_device_ids=true | all-gather | bytes 3456 | tf_op jit(solution)/shard_map/all_gather | solution.py:76
  120.2 16.2 %all-gather.4 = bf16[8,96,2]{1,2,0:T(2,128)(2,1)S(1)} all-gather(bf16[1,96,2]{1,2,0:T(2,128)(2,1)S(1)} %bitcast.126), channel_id=1, replica_groups=mesh['dp'=8,'ctx'=2,'tp'=2] {'dp'}, dimensions={0}, use_global_device_ids=true | all-gather | bytes 3456 | tf_op jit(solution)/shard_map/all_gather | solution.py:77
  139.0 34.7 %all-gather.11.cloned.1.call-done = bf16[768,1536]{1,0:T(8,128)(2,1)} async-done(((bf16[96,1536]{1,0:T(8,128)(2,1)}), bf16[768,1536]{1,0:T(8,128)(2,1)}) %all-gather.11.cloned.1.call-update) | async-done | bytes 2359312 | tf_op jit(solution)/shard_map/all_gather | solution.py:74
  173.7 2.7 fusion.46
  176.4 50.2 %all-gather.13.cloned.1.call-done = bf16[1536,768]{0,1:T(8,128)(2,1)} async-done(((bf16[1536,96]{0,1:T(8,128)(2,1)}), bf16[1536,768]{0,1:T(8,128)(2,1)}) %all-gather.13.cloned.1.call-update) | async-done | bytes 2359312 | tf_op jit(solution)/shard_map/all_gather | solution.py:75
  226.6 3.5 convolution_convert_fusion.5
  230.3 17.0 %all-reduce.9.cloned.1.call-done = bf16[256,768]{1,0:T(8,128)(2,1)} async-done(((bf16[256,768]{1,0:T(8,128)(2,1)}), bf16[256,768]{1,0:T(8,128)(2,1)}) %all-reduce.9.cloned.1.call-update) | async-done | bytes 393232 | tf_op jit(solution)/shard_map/psum | solution.py:124
  251.1 1.4 fusion.8
  254.3 2.5 all-gather.2
  260.6 5.8 multiply_reduce_fusion
  266.5 2.1 multiply_convert_fusion
  268.7 3.6 fusion.55
  272.5 21.6 %scatter_fusion = f32[8,64,6,64]{3,1,2,0:T(8,128)S(1)} fusion(f32[8,64,6,64]{3,1,2,0:T(8,128)S(1)} %broadcast_in_dim.38.clone.1, s32[192]{0:T(256)S(1)} %reshape.312, f32[192,64,64]{2,1,0:T(8,128)} %bitcast.110), kind=kCustom, calls=%fused_computation.2 | custom fusion | flops 786432 | bytes 9438720 | tf_op jit(solution)/shard_map/scatter-add | solution.py:162
  296.3 6.8 fusion.24
  303.3 21.7 %scatter_fusion.1 = f32[8,64,6,64]{3,1,2,0:T(8,128)S(1)} fusion(f32[8,64,6,64]{3,1,2,0:T(8,128)S(1)} %broadcast_in_dim.38.clone, s32[192]{0:T(256)S(1)} %reshape.312, f32[192,64,64]{2,1,0:T(8,128)} %bitcast.109), kind=kCustom, calls=%fused_computation.3 | custom fusion | flops 786432 | bytes 9438720 | tf_op jit(solution)/shard_map/scatter-add | solution.py:167
  325.1 1.5 copy.123
  326.6 2.5 reshape.345
  329.4 3.8 fusion.13
  334.9 8.7 %reduce-scatter.17.cloned.1.call-done = bf16[256,384]{1,0:T(8,128)(2,1)} async-done(((bf16[512,384]{1,0:T(8,128)(2,1)}), bf16[256,384]{1,0:T(8,128)(2,1)}) %reduce-scatter.17.cloned.1.call-update) | async-done | bytes 196624 | tf_op jit(solution)/shard_map/reduce_scatter | solution.py:174
  343.6 1.7 convert_bitcast_fusion
  345.3 3.4 copy.124
  348.6 3.3 copy.133
  353.4 3.8 convolution_convert_fusion
  358.5 2.4 convolution_convert_fusion.1
  363.4 3.0 fusion.9
  366.5 51.8 %reduce-scatter.25.cloned.1.call-done = bf16[96,1152]{1,0:T(8,128)(2,1)} async-done(((bf16[768,1152]{1,0:T(8,128)(2,1)}), bf16[96,1152]{1,0:T(8,128)(2,1)}) %reduce-scatter.25.cloned.1.call-update) | async-done | bytes 221200
  420.2 63.3 %reduce-scatter.19.cloned.1.call-done = bf16[384,96]{0,1:T(8,128)(2,1)} async-done(((bf16[384,768]{0,1:T(8,128)(2,1)}), bf16[384,96]{0,1:T(8,128)(2,1)}) %reduce-scatter.19.cloned.1.call-update) | async-done | bytes 73744 | tf_op jit(solution)/shard_map/reduce_scatter | solution.py:189
  483.5 71.4 %reduce-scatter.23.cloned.1.call-done = bf16[1536,96]{0,1:T(8,128)(2,1)} async-done(((bf16[1536,768]{0,1:T(8,128)(2,1)}), bf16[1536,96]{0,1:T(8,128)(2,1)}) %reduce-scatter.23.cloned.1.call-update) | async-done | bytes 294928 | tf_op jit(solution)/shard_map/reduce_scatter | solution.py:195
  555.0 71.5 %reduce-scatter.21.cloned.1.call-done = bf16[96,1536]{1,0:T(8,128)(2,1)} async-done(((bf16[768,1536]{1,0:T(8,128)(2,1)}), bf16[96,1536]{1,0:T(8,128)(2,1)}) %reduce-scatter.21.cloned.1.call-update) | async-done | bytes 294928 | tf_op jit(solution)/shard_map/reduce_scatter | solution.py:192
  626.5 63.8 %reduce-scatter.27.cloned.1.call-done = bf16[96,2]{1,0:T(8,128)(2,1)} async-done(((bf16[768,2]{1,0:T(8,128)(2,1)}), bf16[96,2]{1,0:T(8,128)(2,1)}) %reduce-scatter.27.cloned.1.call-update) | async-done | bytes 400
  691.2 62.6 %reduce-scatter.29.cloned.1.call-done = bf16[96,2]{1,0:T(8,128)(2,1)} async-done(((bf16[768,2]{1,0:T(8,128)(2,1)}), bf16[96,2]{1,0:T(8,128)(2,1)}) %reduce-scatter.29.cloned.1.call-update) | async-done | bytes 400
  754.6 4.9 all-reduce
  760.7 13.4 %all-reduce.11.cloned.1.call-done = bf16[256,768]{1,0:T(8,128)(2,1)} async-done(((bf16[256,768]{1,0:T(8,128)(2,1)}), bf16[256,768]{1,0:T(8,128)(2,1)}) %all-reduce.11.cloned.1.call-update) | async-done | bytes 393232 | tf_op jit(solution)/shard_map/psum | solution.py:180
  774.1 1.9 add_convert_fusion
  776.0 41.0 %all-reduce.13.cloned.1.call-done = (bf16[3,96,384]{1,2,0:T(8,128)(2,1)}, bf16[384,96]{0,1:T(8,128)(2,1)}, bf16[96,1536]{1,0:T(8,128)(2,1)}, bf16[1536,96]{0,1:T(8,128)(2,1)}) async-done(((bf16[3,96,384]{1,2,0:T(8,128)(2,1)}, bf16[384,96]{0,1:T(8,128)(2,1)}, bf16[96,1536]{1,0:T(8,128)(2,1)}, bf16[1536,96]{0,1:T(8,128)(2,1)}), (bf16[3,96,384]{1,2,0:T(8,128)(2,1)}, bf16[384,96]{0,1:T(8,128)(2,1)}, ...) | async-done | bytes 884752 | tf_op jit(solution)/shard_map/psum | solution.py:206
  817.0 1.9 convert_element_type.212
  818.9 1.8 convert_element_type.214
  820.7 1.9 copy.101
  (196 shorter events, 38.3 us)
Async XLA Ops:
  7.2 53.4 %all-gather.9.cloned.1.call-start = ((), (), s32[]{:S(2)}) async-start(), calls=%async_computation.8 | async-start | bytes 1990656 | tf_op jit(solution)/shard_map/all_gather | solution.py:72
  7.9 128.6 %all-reduce.7.cloned.1.call-start = ((), (), s32[]{:S(2)}) async-start(), calls=%async_computation.9 | async-start | bytes 786432 | tf_op jit(solution)/shard_map/psum | solution.py:115
  72.6 3.4 copy-start.12
  76.0 1.7 copy-start.1
  77.7 2.7 copy-start
  77.7 2.7 copy-start.20
  91.9 6.2 copy-start.11
  97.5 3.2 copy-start.32
  97.5 22.7 %copy-start.33 = (bf16[2,96]{1,0:T(2,128)(2,1)S(1)}, bf16[2,96]{1,0:T(2,128)(2,1)}, u32[]{:S(2)}) copy-start(bf16[2,96]{1,0:T(2,128)(2,1)} %param.16) | copy-start | bytes 1156
  97.5 39.0 %copy-start.4 = (bf16[256,768]{1,0:T(8,128)(2,1)S(1)}, bf16[256,768]{1,0:T(8,128)(2,1)}, u32[]{:S(2)}) copy-start(bf16[256,768]{1,0:T(8,128)(2,1)} %param.10) | copy-start | bytes 1179652
  98.1 78.3 %copy-start.16 = (bf16[256,384]{0,1:T(8,128)(2,1)}, bf16[256,384]{0,1:T(8,128)(2,1)S(1)}, u32[]{:S(2)}) copy-start(bf16[256,384]{0,1:T(8,128)(2,1)S(1)} %convert_element_type.178) | copy-start | bytes 589828
  99.3 74.4 %all-gather.11.cloned.1.call-start = ((), (), s32[]{:S(2)}) async-start(), calls=%async_computation.10 | async-start | bytes 2654208 | tf_op jit(solution)/shard_map/all_gather | solution.py:74
  100.1 126.6 %all-gather.13.cloned.1.call-start = ((), (), s32[]{:S(2)}) async-start(), calls=%async_computation.11 | async-start | bytes 2654208 | tf_op jit(solution)/shard_map/all_gather | solution.py:75
  100.6 146.7 %all-reduce.9.cloned.1.call-start = ((), (), s32[]{:S(2)}) async-start(), calls=%async_computation.12 | async-start | bytes 786432 | tf_op jit(solution)/shard_map/psum | solution.py:124
  139.0 119.1 %copy-start.23 = (f32[256]{0:T(256)}, f32[256]{0:T(256)S(1)}, u32[]{:S(2)}) copy-start(f32[256]{0:T(256)S(1)} %fusion.36) | copy-start | bytes 3076
  176.4 50.2 %copy-start.38 = (f32[256,1536]{1,0:T(8,128)}, f32[256,1536]{1,0:T(8,128)S(1)}, u32[]{:S(2)}) copy-start(f32[256,1536]{1,0:T(8,128)S(1)} %fusion.46) | copy-start | bytes 4718596
  176.4 53.8 %copy-start.22 = (s32[4,6,8,1]{2,1,0,3:T(8,128)S(1)}, s32[4,6,8,1]{2,1,0,3:T(8,128)}, u32[]{:S(2)}) copy-start(s32[4,6,8,1]{2,1,0,3:T(8,128)} %get-tuple-element.67) | copy-start | bytes 2308
  176.4 70.9 %copy-start.5 = (bf16[256,768]{1,0:T(8,128)(2,1)S(1)}, bf16[256,768]{1,0:T(8,128)(2,1)}, u32[]{:S(2)}) copy-start(bf16[256,768]{1,0:T(8,128)(2,1)} %all-reduce.7.cloned.1.call-done) | copy-start | bytes 1179652
  230.1 18.9 %copy-start.14 = (bf16[256,768]{1,0:T(8,128)(2,1)S(1)}, bf16[256,768]{1,0:T(8,128)(2,1)}, u32[]{:S(2)}) copy-start(bf16[256,768]{1,0:T(8,128)(2,1)} %param.19) | copy-start | bytes 1179652
  230.1 104.8 %reduce-scatter.15.cloned.1.call-start = ((), (), s32[]{:S(2)}) async-start(), calls=%async_computation.13 | async-start | bytes 589824 | tf_op jit(solution)/shard_map/reduce_scatter | solution.py:171
  248.7 2.4 copy-start.35
  248.7 2.3 copy-start.39
  251.1 7.0 copy-start.9
  251.1 7.0 copy-start.27
  251.1 2.4 copy-start.34
  258.6 1.7 copy-start.25
  260.3 6.2 slice-start
  260.6 5.9 slice-start.1
  266.5 2.2 copy-start.13
  268.7 3.6 copy-start.3
  296.2 47.3 %reduce-scatter.17.cloned.1.call-start = ((), (), s32[]{:S(2)}) async-start(), calls=%async_computation.14 | async-start | bytes 589824 | tf_op jit(solution)/shard_map/reduce_scatter | solution.py:174
  325.1 4.3 copy-start.2
  329.1 89.1 %reduce-scatter.25.cloned.1.call-start = ((), (), s32[]{:S(2)}) async-start(), calls=%async_computation.19 | async-start | bytes 1990656
  348.6 3.4 copy-start.8
  348.6 3.4 copy-start.17
  348.6 3.4 copy-start.26
  351.9 131.6 %reduce-scatter.19.cloned.1.call-start = ((), (), s32[]{:S(2)}) async-start(), calls=%async_computation.16 | async-start | bytes 663552 | tf_op jit(solution)/shard_map/reduce_scatter | solution.py:189
  353.4 201.6 %reduce-scatter.23.cloned.1.call-start = ((), (), s32[]{:S(2)}) async-start(), calls=%async_computation.18 | async-start | bytes 2654208 | tf_op jit(solution)/shard_map/reduce_scatter | solution.py:195
  357.3 3.7 copy-start.15
  357.3 269.2 %reduce-scatter.21.cloned.1.call-start = ((), (), s32[]{:S(2)}) async-start(), calls=%async_computation.17 | async-start | bytes 2654208 | tf_op jit(solution)/shard_map/reduce_scatter | solution.py:192
  360.9 1.6 copy-start.30
  360.9 2.6 copy-start.36
  360.9 2.6 copy-start.37
  360.9 329.5 %reduce-scatter.27.cloned.1.call-start = ((), (), s32[]{:S(2)}) async-start(), calls=%async_computation.20 | async-start | bytes 221184
  362.4 391.4 %reduce-scatter.29.cloned.1.call-start = ((), (), s32[]{:S(2)}) async-start(), calls=%async_computation.21 | async-start | bytes 221184
  363.4 410.7 %all-reduce.11.cloned.1.call-start = ((), (), s32[]{:S(2)}) async-start(), calls=%async_computation.15 | async-start | bytes 786432 | tf_op jit(solution)/shard_map/psum | solution.py:180
  366.4 450.6 %all-reduce.13.cloned.1.call-start = ((), (), s32[]{:S(2)}) async-start(), calls=%async_computation.22 | async-start | bytes 1916928 | tf_op jit(solution)/shard_map/psum | solution.py:206
  817.0 5.6 copy-start.21
  (9 other events, 9.7 us)
Sparse Core Ops, SparseCore 0:
  10.2 50.3 all-gather.8
  99.4 18.4 all-reduce.6
  120.4 53.2 all-gather.10
  176.0 50.6 all-gather.12
  230.3 17.0 all-reduce.8
  296.4 14.2 reduce-scatter.14
  329.3 14.2 reduce-scatter.16
  352.1 66.1 reduce-scatter.24
  422.5 61.0 reduce-scatter.18
  486.9 68.0 reduce-scatter.22
  558.5 67.9 reduce-scatter.20
  630.2 60.1 reduce-scatter.26
  693.6 60.1 reduce-scatter.28
  756.6 17.4 all-reduce.10
  777.2 39.7 all-reduce.12
